TPU v7x, 256 devices: a whole 4x4x8 slice. The times are simulated.
256 devices in a mesh: seq: 64 (over z, x, core), head: 4 (over y).
Axes of the slice: x: 4, y: 4, z: 8, core: 2. Of those that a mesh axis runs over, the one named last changes fastest.
Arguments:
- qk: bfloat16 [65536, 2048], P('seq', 'head'), may hold values from -8 to 8
- values: bfloat16 [65536, 2048], P('seq', 'head'), may hold values from -6 to 6
- out_weight: bfloat16 [2048, 2048], P('head'), may hold values from -0.125 to 0.125
- out_cotangent: bfloat16 [65536, 2048], P('seq', 'head'), may hold values from -6 to 6
- cluster_ids: int32 [512, 16], P(None, 'head'), may hold values from 0 to 127, as said below
Outputs:
- output: bfloat16 [65536, 2048], P('seq', 'head')
- grad_qk: bfloat16 [65536, 2048], P('seq', 'head')
- grad_values: bfloat16 [65536, 2048], P('seq', 'head')
Inputs may be any that keep to these rules, and one draw needn't show every extreme that they name: `cluster_ids`: call c // 2 the owner of cluster c. Over the blocks of one seq index and the heads of one head index, at most 2 name clusters of one owner, and exactly 2 for some owner. For every head, the clusters of each owner hold exactly 8 blocks together, and some cluster holds all 8.
All inputs are finite; a program needn't handle non-finite values.
Results may differ from a plain program's by a relative error of at most 0.013.
Values may be sent and summed in bfloat16 or wider, within the bound.
A program may use at most 128 MiB of HBM per device.

v0:
```python
import jax
import jax.numpy as jnp
from jax import lax
from jax.sharding import PartitionSpec as P

BLOCK = 128
CL_OWN = 2
NEG_FILL = -1e30


def unit_forward(tokens_x, tokens_v, group):
    row_count = tokens_x.shape[0]
    block_rows = row_count // group.shape[0]
    inv_root = tokens_x.shape[1] ** (-0.5)
    scores = (
        jnp.einsum("rd,cd->rc", tokens_x, tokens_x, preferred_element_type=jnp.float32) * inv_root
    )
    row_group = jnp.repeat(group, block_rows)
    position = jnp.arange(row_count)
    allowed = (row_group[:, None] == row_group[None, :]) & (position[:, None] != position[None, :])
    scores = jnp.where(allowed, scores, NEG_FILL)
    row_max = jnp.max(scores, axis=1, keepdims=True)
    raised = jnp.exp(scores - row_max)
    weights = raised / jnp.sum(raised, axis=1, keepdims=True)
    attended = jnp.einsum(
        "rc,cd->rd", weights.astype(jnp.bfloat16), tokens_v, preferred_element_type=jnp.float32
    )
    return (weights, attended)


def unit_backward(tokens_x, tokens_v, grad_rows, weights, attended):
    inv_root = tokens_x.shape[1] ** (-0.5)
    grad_weights = jnp.einsum("rd,cd->rc", grad_rows, tokens_v, preferred_element_type=jnp.float32)
    row_delta = jnp.sum(grad_rows.astype(jnp.float32) * attended, axis=1, keepdims=True)
    grad_scores = weights * (grad_weights - row_delta)
    symmetric = (grad_scores + grad_scores.T).astype(jnp.bfloat16)
    grad_x = (
        jnp.einsum("rc,cd->rd", symmetric, tokens_x, preferred_element_type=jnp.float32) * inv_root
    ).astype(jnp.bfloat16)
    grad_v = jnp.einsum(
        "rc,rd->cd", weights.astype(jnp.bfloat16), grad_rows, preferred_element_type=jnp.float32
    ).astype(jnp.bfloat16)
    return (grad_x, grad_v)


def forward_unit(operands):
    tokens_x, tokens_v, group = operands
    return unit_forward(tokens_x, tokens_v, group)


def backward_unit(operands):
    tokens_x, tokens_v, grad_rows, weights, attended = operands
    return unit_backward(tokens_x, tokens_v, grad_rows, weights, attended)


def to_slots(local, packing, seq_count):
    blocks_here = packing.shape[1]
    heads_here = packing.shape[2]
    head_width = local.shape[1] // heads_here
    shaped = local.reshape(blocks_here, BLOCK, heads_here, head_width)
    packed = jnp.einsum(
        "ptk,trkd->prd", packing, shaped, preferred_element_type=jnp.float32
    ).astype(jnp.bfloat16)
    return packed.reshape(seq_count, -1, head_width)


def from_slots(arrived, packing):
    head_width = arrived.shape[-1]
    flat = arrived.reshape(packing.shape[0], BLOCK, head_width)
    placed = jnp.einsum("ptk,prd->trkd", packing, flat, preferred_element_type=jnp.float32).astype(
        jnp.bfloat16
    )
    return placed.reshape(packing.shape[1] * BLOCK, packing.shape[2] * head_width)


def to_units(arrived, picking, unit_count):
    head_width = arrived.shape[-1]
    flat = arrived.reshape(picking.shape[1], BLOCK, head_width)
    gathered = jnp.einsum("up,prd->urd", picking, flat, preferred_element_type=jnp.float32).astype(
        jnp.bfloat16
    )
    return gathered.reshape(unit_count, -1, head_width)


def from_units(results, picking, seq_count):
    head_width = results.shape[-1]
    flat = results.reshape(picking.shape[0], BLOCK, head_width)
    placed = jnp.einsum("up,urd->prd", picking, flat, preferred_element_type=jnp.float32).astype(
        jnp.bfloat16
    )
    return placed.reshape(seq_count, -1, head_width)


def model_output(attended, out_weight):
    partial_term = jnp.dot(attended, out_weight, preferred_element_type=jnp.float32)
    return lax.psum_scatter(
        partial_term.astype(jnp.bfloat16), "head", scatter_dimension=1, tiled=True
    )


def cotangent_heads(out_cotangent, out_weight):
    summed = jnp.einsum(
        "tn,kn->tk",
        lax.all_gather(out_cotangent, "head", axis=1, tiled=True),
        out_weight,
        preferred_element_type=jnp.float32,
    )
    return summed.astype(jnp.bfloat16)


def per_device(qk, values, out_weight, out_cotangent, cluster_ids):
    seq_count = lax.axis_size("seq")
    my_seq = lax.axis_index("seq")
    block_count = cluster_ids.shape[0]
    heads_here = cluster_ids.shape[1]
    blocks_here = qk.shape[0] // BLOCK
    item_count = blocks_here * heads_here
    per_peer = max(2, (item_count + seq_count - 1) // seq_count)
    slot_total = seq_count * per_peer
    owners = cluster_ids // CL_OWN
    item_owner = owners.reshape(seq_count, item_count)
    item_order = jnp.arange(item_count)
    before = item_order[None, :] < item_order[:, None]
    same_owner = item_owner[:, :, None] == item_owner[:, None, :]
    rank_sent = jnp.sum((same_owner & before[None, :, :]).astype(jnp.int32), axis=2)
    slot_index = item_owner * per_peer + rank_sent
    my_slots = lax.dynamic_index_in_dim(slot_index, my_seq, 0, keepdims=False)
    slot_range = jnp.arange(slot_total, dtype=jnp.int32)
    packing = (
        (slot_range[:, None] == my_slots[None, :])
        .astype(jnp.bfloat16)
        .reshape(slot_total, blocks_here, heads_here)
    )
    source_seq = jnp.arange(seq_count, dtype=jnp.int32)[:, None]
    arrival_slot = source_seq * per_peer + rank_sent
    received = (owners == my_seq).T.astype(jnp.int32)
    source_slot = arrival_slot.reshape(block_count, heads_here).T
    position = jnp.cumsum(received, axis=1) - received
    places = jnp.arange(blocks_here, dtype=jnp.int32)
    chosen = (received[:, None, :] == 1) & (position[:, None, :] == places[None, :, None])
    unit_slot = jnp.sum(jnp.where(chosen, source_slot[:, None, :], 0), axis=2)
    unit_group = jnp.sum(jnp.where(chosen, cluster_ids.T[:, None, :], 0), axis=2)
    picking = (unit_slot.reshape(-1)[:, None] == slot_range[None, :]).astype(jnp.bfloat16)
    send_x = to_slots(qk, packing, seq_count)
    send_v = to_slots(values, packing, seq_count)
    arrived_x, arrived_v = (
        lax.all_to_all(send_x, "seq", split_axis=0, concat_axis=0, tiled=True),
        lax.all_to_all(send_v, "seq", split_axis=0, concat_axis=0, tiled=True),
    )
    unit_x = to_units(arrived_x, picking, heads_here)
    unit_v = to_units(arrived_v, picking, heads_here)
    weights, unit_att = lax.map(forward_unit, (unit_x, unit_v, unit_group))
    home_att = lax.all_to_all(
        from_units(unit_att.astype(jnp.bfloat16), picking, seq_count),
        "seq",
        split_axis=0,
        concat_axis=0,
        tiled=True,
    )
    attended = from_slots(home_att, packing)
    output = model_output(attended, out_weight)
    grad_attended = cotangent_heads(out_cotangent, out_weight)
    arrived_g = lax.all_to_all(
        to_slots(grad_attended, packing, seq_count), "seq", split_axis=0, concat_axis=0, tiled=True
    )
    unit_g = to_units(arrived_g, picking, heads_here)
    unit_gx, unit_gv = lax.map(backward_unit, (unit_x, unit_v, unit_g, weights, unit_att))
    home_gx, home_gv = (
        lax.all_to_all(
            from_units(unit_gx, picking, seq_count), "seq", split_axis=0, concat_axis=0, tiled=True
        ),
        lax.all_to_all(
            from_units(unit_gv, picking, seq_count), "seq", split_axis=0, concat_axis=0, tiled=True
        ),
    )
    grad_qk = from_slots(home_gx, packing)
    grad_values = from_slots(home_gv, packing)
    return (output, grad_qk, grad_values)


def solution(mesh):
    return jax.shard_map(
        per_device,
        mesh=mesh,
        in_specs=(
            P("seq", "head"),
            P("seq", "head"),
            P("head", None),
            P("seq", "head"),
            P(None, "head"),
        ),
        out_specs=(P("seq", "head"), P("seq", "head"), P("seq", "head")),
        check_vma=False,
    )
```

profile of v0, /device:TPU:16, one launch (start us, length us, event | category | flops | bytes accessed | tf_op | source)
XLA Modules:
  0.0 683.7 jit_solution(4577155340845065639)
XLA Ops:
  11.8 4.6 copy.60
  16.4 12.2 %all-to-all-start = ((bf16[64,256,128]{2,1,0:T(8,128)(2,1)}), bf16[64,256,128]{2,1,0:T(8,128)(2,1)}, u32[]{:S(2)}, u32[]{:S(2)}) async-start(bf16[64,256,128]{2,1,0:T(8,128)(2,1)} %bitcast.193), calls=%async_computation | async-start | bytes 8388608 | tf_op jit(solution)/shard_map/all_to_all | solution.py:147
  31.4 4.7 copy.64
  36.0 88.8 %all-to-all-done = bf16[64,256,128]{2,1,0:T(8,128)(2,1)} async-done(((bf16[64,256,128]{2,1,0:T(8,128)(2,1)}), bf16[64,256,128]{2,1,0:T(8,128)(2,1)}, u32[]{:S(2)}, u32[]{:S(2)}) %all-to-all-start) | async-done | bytes 4194336 | tf_op jit(solution)/shard_map/all_to_all | solution.py:147
  124.8 5.8 all-to-all-start.1
  134.1 50.2 %all-gather.2.cloned.1.call-done = bf16[1024,2048]{1,0:T(8,128)(2,1)} async-done(((bf16[1024,512]{1,0:T(8,128)(2,1)}), bf16[1024,2048]{1,0:T(8,128)(2,1)}) %all-gather.2.cloned.1.call-update) | async-done | bytes 4194320 | tf_op jit(solution)/shard_map/all_gather | solution.py:104
  184.3 5.5 convolution_convert_fusion.4
  192.6 4.6 copy.73
  197.2 4.8 fusion.70
  202.4 24.5 %all-to-all-done.1 = bf16[64,256,128]{2,1,0:T(8,128)(2,1)} async-done(((bf16[64,256,128]{2,1,0:T(8,128)(2,1)}), bf16[64,256,128]{2,1,0:T(8,128)(2,1)}, u32[]{:S(2)}, u32[]{:S(2)}) %all-to-all-start.1) | async-done | bytes 4194336 | tf_op jit(solution)/shard_map/all_to_all | solution.py:148
  226.9 6.1 all-to-all-start.3
  233.0 4.8 fusion.73
  239.2 27.8 %while.24 = (s32[]{:T(128)}, f32[4,1024,1024]{1,2,0:T(8,128)}, f32[4,1024,128]{2,1,0:T(8,128)}, s32[4,8]{1,0:T(4,128)S(1)}, bf16[4,1024,128]{2,1,0:T(8,128)(2,1)S(1)}, /*index=5*/bf16[4,1024,128]{2,1,0:T(8,128)(2,1)}, s32[]{:T(128)}) while((s32[]{:T(128)}, f32[4,1024,1024]{1,2,0:T(8,128)}, f32[4,1024,128]{2,1,0:T(8,128)}, ...), condition=%wide.region_8.9_spmd, body=%wide.region_5.8_spmd.sunk | while | flops 550500352 | bytes 22062772 | solution.py:152
  270.4 4.7 copy.68
  275.1 54.1 %all-to-all-done.3 = bf16[64,256,128]{2,1,0:T(8,128)(2,1)} async-done(((bf16[64,256,128]{2,1,0:T(8,128)(2,1)}), bf16[64,256,128]{2,1,0:T(8,128)(2,1)}, u32[]{:S(2)}, u32[]{:S(2)}) %all-to-all-start.3) | async-done | bytes 4194336 | tf_op jit(solution)/shard_map/all_to_all | solution.py:163
  329.2 5.8 all-to-all-start.2
  335.0 4.8 fusion.76
  340.3 112.8 %while.25 = (s32[]{:T(128)}, bf16[4,1024,128]{2,1,0:T(8,128)(2,1)}, bf16[4,1024,128]{2,1,0:T(8,128)(2,1)}, f32[4,1024,1024]{1,2,0:T(8,128)}, bf16[4,1024,128]{2,...) while((s32[]{:T(128)}, bf16[4,1024,128]{2,1,0:T(8,128)(2,1)}, ...), condition=%wide.region_12.13_spmd, body=%wide.region_10.12_spmd.sunk | while | flops 811334656 | bytes 65285248 | solution.py:167
  341.5 4.7 constant_dynamic-slice_fusion.3
  346.3 5.3 copy.159
  351.6 4.9 bitcast_multiply_fusion.3
  356.5 5.4 copy.160
  361.9 5.1 fusion.168
  369.7 4.7 constant_dynamic-slice_fusion.3
  374.5 5.3 copy.159
  379.8 4.9 bitcast_multiply_fusion.3
  384.7 5.4 copy.160
  390.1 5.1 fusion.168
  397.9 4.7 constant_dynamic-slice_fusion.3
  402.7 5.3 copy.159
  408.0 4.9 bitcast_multiply_fusion.3
  412.9 5.4 copy.160
  418.3 5.1 fusion.168
  426.1 4.7 constant_dynamic-slice_fusion.3
  430.9 5.3 copy.159
  436.2 4.9 bitcast_multiply_fusion.3
  441.1 5.4 copy.160
  446.5 5.1 fusion.168
  455.7 4.7 copy.78
  460.4 10.9 %all-to-all-start.4 = ((bf16[64,256,128]{2,1,0:T(8,128)(2,1)}), bf16[64,256,128]{2,1,0:T(8,128)(2,1)}, u32[]{:S(2)}, u32[]{:S(2)}) async-start(bf16[64,256,128]{2,1,0:T(8,128)(2,1)} %bitcast.192), calls=%async_computation.5 | async-start | bytes 8388608 | tf_op jit(solution)/shard_map/all_to_all | solution.py:169
  473.8 4.7 copy.82
  478.5 88.9 %all-to-all-done.4 = bf16[64,256,128]{2,1,0:T(8,128)(2,1)} async-done(((bf16[64,256,128]{2,1,0:T(8,128)(2,1)}), bf16[64,256,128]{2,1,0:T(8,128)(2,1)}, u32[]{:S(2)}, u32[]{:S(2)}) %all-to-all-start.4) | async-done | bytes 4194336 | tf_op jit(solution)/shard_map/all_to_all | solution.py:169
  567.5 5.8 all-to-all-start.5
  573.3 4.8 fusion.94
  580.1 5.6 convolution_convert_fusion
  585.7 4.8 fusion.91
  591.0 78.5 %all-to-all-done.5 = bf16[64,256,128]{2,1,0:T(8,128)(2,1)} async-done(((bf16[64,256,128]{2,1,0:T(8,128)(2,1)}), bf16[64,256,128]{2,1,0:T(8,128)(2,1)}, u32[]{:S(2)}, u32[]{:S(2)}) %all-to-all-start.5) | async-done | bytes 4194336 | tf_op jit(solution)/shard_map/all_to_all | solution.py:172
  669.5 4.8 fusion.88
  (101 shorter events, 67.6 us)
Async XLA Ops:
  7.2 177.1 %copy-start = (bf16[512,2048]{1,0:T(8,128)(2,1)S(1)}, bf16[512,2048]{1,0:T(8,128)(2,1)}, u32[]{:S(2)}) copy-start(bf16[512,2048]{1,0:T(8,128)(2,1)} %param.11) | copy-start | bytes 6291460
  9.0 182.1 %copy-start.3 = (s32[8,4]{0,1:T(4,128)}, s32[8,4]{0,1:T(4,128)S(1)}, u32[]{:S(2)}) copy-start(s32[8,4]{0,1:T(4,128)S(1)} %copy.58) | copy-start | bytes 388
  16.4 108.4 %all-to-all-start = ((bf16[64,256,128]{2,1,0:T(8,128)(2,1)}), bf16[64,256,128]{2,1,0:T(8,128)(2,1)}, u32[]{:S(2)}, u32[]{:S(2)}) async-start(bf16[64,256,128]{2,1,0:T(8,128)(2,1)} %bitcast.193), calls=%async_computation | async-start | bytes 8388608 | tf_op jit(solution)/shard_map/all_to_all | solution.py:147
  124.8 8.9 %copy-start.5 = (s32[512,4]{0,1:T(4,128)S(1)}, s32[512,4]{0,1:T(4,128)}, u32[]{:S(2)}) copy-start(s32[512,4]{0,1:T(4,128)} %param.13) | copy-start | bytes 24580
  124.8 102.0 %all-to-all-start.1 = ((bf16[64,256,128]{2,1,0:T(8,128)(2,1)}), bf16[64,256,128]{2,1,0:T(8,128)(2,1)}, u32[]{:S(2)}, u32[]{:S(2)}) async-start(bf16[64,256,128]{2,1,0:T(8,128)(2,1)} %bitcast.190), calls=%async_computation.1 | async-start | bytes 8388608 | tf_op jit(solution)/shard_map/all_to_all | solution.py:148
  130.6 53.7 %all-gather.2.cloned.1.call-start = ((), (), s32[]{:S(2)}) async-start(), calls=%async_computation.8 | async-start | bytes 5242880 | tf_op jit(solution)/shard_map/all_gather | solution.py:104
  226.9 102.3 %all-to-all-start.3 = ((bf16[64,256,128]{2,1,0:T(8,128)(2,1)}), bf16[64,256,128]{2,1,0:T(8,128)(2,1)}, u32[]{:S(2)}, u32[]{:S(2)}) async-start(bf16[64,256,128]{2,1,0:T(8,128)(2,1)} %bitcast.188), calls=%async_computation.4 | async-start | bytes 8388608 | tf_op jit(solution)/shard_map/all_to_all | solution.py:163
  266.9 3.5 copy-start.2
  329.2 131.2 %all-to-all-start.2 = ((bf16[64,256,128]{2,1,0:T(8,128)(2,1)}), bf16[64,256,128]{2,1,0:T(8,128)(2,1)}, u32[]{:S(2)}, u32[]{:S(2)}) async-start(bf16[64,256,128]{2,1,0:T(8,128)(2,1)} %bitcast.189), calls=%async_computation.2 | async-start | bytes 8388608 | tf_op jit(solution)/shard_map/all_to_all | solution.py:153
  361.9 5.1 copy-start.1
  390.1 5.1 copy-start.1
  418.3 5.1 copy-start.1
  446.5 5.1 copy-start.1
  460.4 107.1 %all-to-all-start.4 = ((bf16[64,256,128]{2,1,0:T(8,128)(2,1)}), bf16[64,256,128]{2,1,0:T(8,128)(2,1)}, u32[]{:S(2)}, u32[]{:S(2)}) async-start(bf16[64,256,128]{2,1,0:T(8,128)(2,1)} %bitcast.192), calls=%async_computation.5 | async-start | bytes 8388608 | tf_op jit(solution)/shard_map/all_to_all | solution.py:169
  567.4 5.9 copy-start.4
  567.5 102.0 %all-to-all-start.5 = ((bf16[64,256,128]{2,1,0:T(8,128)(2,1)}), bf16[64,256,128]{2,1,0:T(8,128)(2,1)}, u32[]{:S(2)}, u32[]{:S(2)}) async-start(bf16[64,256,128]{2,1,0:T(8,128)(2,1)} %bitcast.191), calls=%async_computation.6 | async-start | bytes 8388608 | tf_op jit(solution)/shard_map/all_to_all | solution.py:172
  573.3 103.2 %reduce-scatter.2.cloned.1.call-start = ((), (), s32[]{:S(2)}) async-start(), calls=%async_computation.7 | async-start | bytes 5242880 | tf_op jit(solution)/shard_map/reduce_scatter | solution.py:96
Sparse Core Ops, SparseCore 0:
  133.3 50.9 all-gather.1
  585.8 48.8 reduce-scatter.1
where the time goes:
time: 694 us; the launch traced here: 684 us
  waiting for transfers between devices  386 us (56%)
  matrix products  111 us (16%)
  local copies, waits for them, and re-layouts  102 us (15%)
  starting transfers between devices  46.9 us (7%)
  other arithmetic  22.8 us (3%)
  between operations  14.8 us (2%)
    all_to_all x1, waiting for transfers between devices, per_device(): lax.all_to_all(from_units(unit_gx, picking, seq_count), 'seq', split_axis...  88.9 us
    all_to_all x1, waiting for transfers between devices, per_device(): lax.all_to_all(send_x, 'seq', split_axis=0, concat_axis=0, tiled=True)  88.8 us
    all_to_all x1, waiting for transfers between devices, per_device(): lax.all_to_all(from_units(unit_gv, picking, seq_count), 'seq', split_axis...  78.5 us
    all_to_all x1, waiting for transfers between devices, per_device(): lax.all_to_all(to_slots(grad_attended, packing, seq_count), 'seq', split_...  54.1 us
    all_gather x1, waiting for transfers between devices, cotangent_heads(): lax.all_gather(out_cotangent, 'head', axis=1, tiled=True)  50.2 us
    dynamic_slice x8, local copies, waits for them, and re-layouts, per_device(): lax.map(backward_unit, (unit_x, unit_v, unit_g, weights, unit_att))  40.2 us
    all_to_all x1, waiting for transfers between devices, per_device(): lax.all_to_all(send_v, 'seq', split_axis=0, concat_axis=0, tiled=True)  24.5 us
    mul x4, local copies, waits for them, and re-layouts, unit_backward(): grad_scores = weights * (grad_weights - row_delta)  21.5 us
  transfers between devices with their start and end apart: 8, of which 6 were waited for; matrix products, arithmetic and copies ran while one was open for 33% of the time, Pallas kernels for 0%

commit v1 on v0

--- a/solution.py
+++ b/solution.py
@@ -101,7 +101,9 @@
 def cotangent_heads(out_cotangent, out_weight):
     summed = jnp.einsum(
         "tn,kn->tk",
-        lax.all_gather(out_cotangent, "head", axis=1, tiled=True),
+        jnp.concatenate(
+            lax.all_to_all(jnp.stack([out_cotangent] * lax.axis_size("head")), "head", 0, 0), axis=1
+        ),
         out_weight,
         preferred_element_type=jnp.float32,
     )

time: 694 us -> 743 us (1.071)
  waiting for transfers between devices: 386 us -> 422 us
    all_to_all x1, waiting for transfers between devices: 24.5 us -> 75.4 us  [per_device(): lax.all_to_all(send_v, 'seq', split_axis=0, concat_axis=0, tiled=True)]
    all_gather x1 -> x0, waiting for transfers between devices: 50.2 us -> none  [cotangent_heads(): lax.all_gather(out_cotangent, 'head', axis=1, tiled=True)]
    all_to_all x0 -> x1, waiting for transfers between devices: none -> 35.9 us  [cotangent_heads(): lax.all_to_all(jnp.stack([out_cotangent] * lax.axis_size('head')), 'head'...]
  transfers between devices with their start and end apart: 8 -> 8, of which waited for: 6 -> 6; matrix products, arithmetic and copies ran while one was open for 33% -> 32% of each run, Pallas kernels for 0% -> 0%
where the time goes in v1:
time: 743 us; the launch traced here: 730 us
  waiting for transfers between devices  422 us (57%)
  matrix products  112 us (15%)
  local copies, waits for them, and re-layouts  106 us (14%)
  starting transfers between devices  53.9 us (7%)
  other arithmetic  22 us (3%)
  between operations  14.7 us (2%)
    all_to_all x1, waiting for transfers between devices, per_device(): lax.all_to_all(from_units(unit_gx, picking, seq_count), 'seq', split_axis...  88.9 us
    all_to_all x1, waiting for transfers between devices, per_device(): lax.all_to_all(send_x, 'seq', split_axis=0, concat_axis=0, tiled=True)  88.8 us
    all_to_all x1, waiting for transfers between devices, per_device(): lax.all_to_all(from_units(unit_gv, picking, seq_count), 'seq', split_axis...  78.5 us
    all_to_all x1, waiting for transfers between devices, per_device(): lax.all_to_all(send_v, 'seq', split_axis=0, concat_axis=0, tiled=True)  75.4 us
    all_to_all x1, waiting for transfers between devices, per_device(): lax.all_to_all(to_slots(grad_attended, packing, seq_count), 'seq', split_...  54.1 us
    dynamic_slice x8, local copies, waits for them, and re-layouts, per_device(): lax.map(backward_unit, (unit_x, unit_v, unit_g, weights, unit_att))  40.2 us
    all_to_all x1, waiting for transfers between devices, cotangent_heads(): lax.all_to_all(jnp.stack([out_cotangent] * lax.axis_size('head')), 'head'...  35.9 us
    mul x4, local copies, waits for them, and re-layouts, unit_backward(): grad_scores = weights * (grad_weights - row_delta)  21.5 us
  transfers between devices with their start and end apart: 8, of which 6 were waited for; matrix products, arithmetic and copies ran while one was open for 32% of the time, Pallas kernels for 0%

profile of v1, /device:TPU:16, one launch (start us, length us, event | category | flops | bytes accessed | tf_op | source)
XLA Modules:
  0.0 730.2 jit_solution(8987655272056433887)
XLA Ops:
  11.3 7.0 all-to-all-start.3
  22.1 4.7 copy.61
  26.7 35.9 %all-to-all-done.3 = bf16[4,1024,512]{1,2,0:T(8,128)(2,1)} async-done(((bf16[4,1024,512]{1,2,0:T(8,128)(2,1)}), bf16[4,1024,512]{1,2,0:T(8,128)(2,1)}, u32[]{:S(2)}, u32[]{:S(2)}) %all-to-all-start.3) | async-done | bytes 4194336 | tf_op jit(solution)/shard_map/all_to_all | solution.py:105
  62.7 12.3 %all-to-all-start = ((bf16[64,256,128]{2,1,0:T(8,128)(2,1)}), bf16[64,256,128]{2,1,0:T(8,128)(2,1)}, u32[]{:S(2)}, u32[]{:S(2)}) async-start(bf16[64,256,128]{2,1,0:T(8,128)(2,1)} %bitcast.196), calls=%async_computation | async-start | bytes 8388608 | tf_op jit(solution)/shard_map/all_to_all | solution.py:149
  77.8 4.7 copy.65
  82.4 88.8 %all-to-all-done = bf16[64,256,128]{2,1,0:T(8,128)(2,1)} async-done(((bf16[64,256,128]{2,1,0:T(8,128)(2,1)}), bf16[64,256,128]{2,1,0:T(8,128)(2,1)}, u32[]{:S(2)}, u32[]{:S(2)}) %all-to-all-start) | async-done | bytes 4194336 | tf_op jit(solution)/shard_map/all_to_all | solution.py:149
  171.2 5.9 all-to-all-start.1
  179.8 5.5 convolution_convert_fusion.4
  192.7 4.8 fusion.70
  198.0 75.4 %all-to-all-done.1 = bf16[64,256,128]{2,1,0:T(8,128)(2,1)} async-done(((bf16[64,256,128]{2,1,0:T(8,128)(2,1)}), bf16[64,256,128]{2,1,0:T(8,128)(2,1)}, u32[]{:S(2)}, u32[]{:S(2)}) %all-to-all-start.1) | async-done | bytes 4194336 | tf_op jit(solution)/shard_map/all_to_all | solution.py:150
  273.3 6.1 all-to-all-start.4
  279.4 4.8 fusion.73
  285.6 27.8 %while.24 = (s32[]{:T(128)}, f32[4,1024,1024]{1,2,0:T(8,128)}, f32[4,1024,128]{2,1,0:T(8,128)}, s32[4,8]{1,0:T(4,128)S(1)}, bf16[4,1024,128]{2,1,0:T(8,128)(2,1)S(1)}, /*index=5*/bf16[4,1024,128]{2,1,0:T(8,128)(2,1)}, s32[]{:T(128)}) while((s32[]{:T(128)}, f32[4,1024,1024]{1,2,0:T(8,128)}, f32[4,1024,128]{2,1,0:T(8,128)}, ...), condition=%wide.region_8.9_spmd, body=%wide.region_5.8_spmd.sunk | while | flops 550500352 | bytes 22062772 | solution.py:154
  316.9 4.7 copy.69
  321.6 54.1 %all-to-all-done.4 = bf16[64,256,128]{2,1,0:T(8,128)(2,1)} async-done(((bf16[64,256,128]{2,1,0:T(8,128)(2,1)}), bf16[64,256,128]{2,1,0:T(8,128)(2,1)}, u32[]{:S(2)}, u32[]{:S(2)}) %all-to-all-start.4) | async-done | bytes 4194336 | tf_op jit(solution)/shard_map/all_to_all | solution.py:165
  375.7 5.8 all-to-all-start.2
  381.5 4.8 fusion.76
  386.7 112.8 %while.25 = (s32[]{:T(128)}, bf16[4,1024,128]{2,1,0:T(8,128)(2,1)}, bf16[4,1024,128]{2,1,0:T(8,128)(2,1)}, f32[4,1024,1024]{1,2,0:T(8,128)}, bf16[4,1024,128]{2,...) while((s32[]{:T(128)}, bf16[4,1024,128]{2,1,0:T(8,128)(2,1)}, ...), condition=%wide.region_12.13_spmd, body=%wide.region_10.12_spmd.sunk | while | flops 811334656 | bytes 65285248 | solution.py:169
  388.0 4.7 constant_dynamic-slice_fusion.3
  392.7 5.3 copy.161
  398.1 4.9 bitcast_multiply_fusion.3
  403.0 5.4 copy.162
  408.4 5.1 fusion.168
  416.2 4.7 constant_dynamic-slice_fusion.3
  421.0 5.3 copy.161
  426.3 4.9 bitcast_multiply_fusion.3
  431.2 5.4 copy.162
  436.6 5.1 fusion.168
  444.4 4.7 constant_dynamic-slice_fusion.3
  449.2 5.3 copy.161
  454.5 4.9 bitcast_multiply_fusion.3
  459.4 5.4 copy.162
  464.8 5.1 fusion.168
  472.6 4.7 constant_dynamic-slice_fusion.3
  477.4 5.3 copy.161
  482.7 4.9 bitcast_multiply_fusion.3
  487.6 5.4 copy.162
  493.0 5.1 fusion.168
  502.2 4.7 copy.80
  506.9 10.9 %all-to-all-start.5 = ((bf16[64,256,128]{2,1,0:T(8,128)(2,1)}), bf16[64,256,128]{2,1,0:T(8,128)(2,1)}, u32[]{:S(2)}, u32[]{:S(2)}) async-start(bf16[64,256,128]{2,1,0:T(8,128)(2,1)} %bitcast.195), calls=%async_computation.6 | async-start | bytes 8388608 | tf_op jit(solution)/shard_map/all_to_all | solution.py:171
  520.4 4.7 copy.84
  525.0 88.9 %all-to-all-done.5 = bf16[64,256,128]{2,1,0:T(8,128)(2,1)} async-done(((bf16[64,256,128]{2,1,0:T(8,128)(2,1)}), bf16[64,256,128]{2,1,0:T(8,128)(2,1)}, u32[]{:S(2)}, u32[]{:S(2)}) %all-to-all-start.5) | async-done | bytes 4194336 | tf_op jit(solution)/shard_map/all_to_all | solution.py:171
  614.0 5.8 all-to-all-start.6
  619.8 4.8 fusion.94
  626.6 5.6 convolution_convert_fusion
  632.2 4.8 fusion.91
  637.5 78.5 %all-to-all-done.6 = bf16[64,256,128]{2,1,0:T(8,128)(2,1)} async-done(((bf16[64,256,128]{2,1,0:T(8,128)(2,1)}), bf16[64,256,128]{2,1,0:T(8,128)(2,1)}, u32[]{:S(2)}, u32[]{:S(2)}) %all-to-all-start.6) | async-done | bytes 4194336 | tf_op jit(solution)/shard_map/all_to_all | solution.py:174
  716.0 4.8 fusion.88
  (102 shorter events, 74.7 us)
Async XLA Ops:
  7.2 172.7 %copy-start = (bf16[512,2048]{1,0:T(8,128)(2,1)S(1)}, bf16[512,2048]{1,0:T(8,128)(2,1)}, u32[]{:S(2)}) copy-start(bf16[512,2048]{1,0:T(8,128)(2,1)} %param.11) | copy-start | bytes 6291460
  11.3 7.0 copy-start.5
  11.3 51.4 %all-to-all-start.3 = ((bf16[4,1024,512]{1,2,0:T(8,128)(2,1)}), bf16[4,1024,512]{1,2,0:T(8,128)(2,1)}, u32[]{:S(2)}, u32[]{:S(2)}) async-start(bf16[4,1024,512]{1,2,0:T(8,128)(2,1)} %stack.2), calls=%async_computation.4 | async-start | bytes 8388608 | tf_op jit(solution)/shard_map/all_to_all | solution.py:105
  19.3 167.4 %copy-start.3 = (s32[8,4]{0,1:T(4,128)}, s32[8,4]{0,1:T(4,128)S(1)}, u32[]{:S(2)}) copy-start(s32[8,4]{0,1:T(4,128)S(1)} %copy.59) | copy-start | bytes 388
  62.7 108.6 %all-to-all-start = ((bf16[64,256,128]{2,1,0:T(8,128)(2,1)}), bf16[64,256,128]{2,1,0:T(8,128)(2,1)}, u32[]{:S(2)}, u32[]{:S(2)}) async-start(bf16[64,256,128]{2,1,0:T(8,128)(2,1)} %bitcast.196), calls=%async_computation | async-start | bytes 8388608 | tf_op jit(solution)/shard_map/all_to_all | solution.py:149
  171.2 102.1 %all-to-all-start.1 = ((bf16[64,256,128]{2,1,0:T(8,128)(2,1)}), bf16[64,256,128]{2,1,0:T(8,128)(2,1)}, u32[]{:S(2)}, u32[]{:S(2)}) async-start(bf16[64,256,128]{2,1,0:T(8,128)(2,1)} %bitcast.193), calls=%async_computation.1 | async-start | bytes 8388608 | tf_op jit(solution)/shard_map/all_to_all | solution.py:150
  273.3 102.3 %all-to-all-start.4 = ((bf16[64,256,128]{2,1,0:T(8,128)(2,1)}), bf16[64,256,128]{2,1,0:T(8,128)(2,1)}, u32[]{:S(2)}, u32[]{:S(2)}) async-start(bf16[64,256,128]{2,1,0:T(8,128)(2,1)} %bitcast.191), calls=%async_computation.5 | async-start | bytes 8388608 | tf_op jit(solution)/shard_map/all_to_all | solution.py:165
  313.4 3.5 copy-start.2
  375.7 131.2 %all-to-all-start.2 = ((bf16[64,256,128]{2,1,0:T(8,128)(2,1)}), bf16[64,256,128]{2,1,0:T(8,128)(2,1)}, u32[]{:S(2)}, u32[]{:S(2)}) async-start(bf16[64,256,128]{2,1,0:T(8,128)(2,1)} %bitcast.192), calls=%async_computation.2 | async-start | bytes 8388608 | tf_op jit(solution)/shard_map/all_to_all | solution.py:155
  408.4 5.1 copy-start.1
  436.6 5.1 copy-start.1
  464.8 5.1 copy-start.1
  493.0 5.1 copy-start.1
  506.9 107.1 %all-to-all-start.5 = ((bf16[64,256,128]{2,1,0:T(8,128)(2,1)}), bf16[64,256,128]{2,1,0:T(8,128)(2,1)}, u32[]{:S(2)}, u32[]{:S(2)}) async-start(bf16[64,256,128]{2,1,0:T(8,128)(2,1)} %bitcast.195), calls=%async_computation.6 | async-start | bytes 8388608 | tf_op jit(solution)/shard_map/all_to_all | solution.py:171
  614.0 5.9 copy-start.4
  614.0 102.0 %all-to-all-start.6 = ((bf16[64,256,128]{2,1,0:T(8,128)(2,1)}), bf16[64,256,128]{2,1,0:T(8,128)(2,1)}, u32[]{:S(2)}, u32[]{:S(2)}) async-start(bf16[64,256,128]{2,1,0:T(8,128)(2,1)} %bitcast.194), calls=%async_computation.7 | async-start | bytes 8388608 | tf_op jit(solution)/shard_map/all_to_all | solution.py:174
  619.8 103.2 %reduce-scatter.2.cloned.1.call-start = ((), (), s32[]{:S(2)}) async-start(), calls=%async_computation.8 | async-start | bytes 5242880 | tf_op jit(solution)/shard_map/reduce_scatter | solution.py:96
Sparse Core Ops, SparseCore 0:
  632.4 49.4 reduce-scatter.1
